TPU v7x, 32 devices: a whole 2x2x4 slice. The times are simulated.
32 devices in a mesh: pole: 2 (over x), wide: 8 (over z, y), narrow: 2 (over core).
Axes of the slice: x: 2, y: 2, z: 4, core: 2. Of those that a mesh axis runs over, the one named last changes fastest.
Arguments:
- h_panel: float32 [512, 2048], P(('pole', 'wide', 'narrow')), parts along dimension 0, may hold values from -0.3 to 0.3
- s_panel: float32 [512, 2048], P(('pole', 'wide', 'narrow')), parts along dimension 0, may hold values from -0.3 to 0.3
- col_index: int32 [512], P('pole'), parts along dimension 0, may hold values from 0 to 255, each once
- pattern: int32 [256], P(('pole', 'wide', 'narrow')), parts along dimension 0, may hold values 0 or 1
- dinv: float32 [512, 256], P('pole'), parts along dimension 0, may hold values from -4 to 4, as said below
- ainv_cc: float32 [4096, 8, 2, 128], P(('pole', 'wide'), None, 'narrow'), parts along dimension 0, may hold values from -1 to 1
Outputs:
- ainv_ck: float32 [4096, 256], P(('pole', 'wide'), 'narrow'), parts along dimension 0
- ainv_kk: float32 [512, 256], P(('pole', 'wide'), 'narrow'), parts along dimension 0
There are 2 independent parts, one for each index of `pole`. A program takes and returns all parts, laid end to end along the dimension named above; each array names one. Nothing has to cross between parts.
Inputs may be any that keep to these rules, and one draw needn't show every extreme that they name: `dinv`: diagonal entries between 0.25 and 4, off-diagonal entries at most 4 / sqrt(256) in magnitude.
All inputs are finite; a program needn't handle non-finite values. No bound on the sum of `pattern` on one device may be relied on, other than what follows from the above.
Results may differ from a plain program's by a relative error of at most 0.00011.
Values sent between devices are 32-bit elements; how exact they have to be, the bound alone decides.
No kernel may reach another device: no remote copies, remote signals or barrier semaphores. Data moves between devices by JAX's collectives and lax.ppermute only.
A program may use at most 64 MiB of HBM per device.

v0:
```python
import jax
import jax.numpy as jnp
from jax import lax
from jax.sharding import PartitionSpec as P

POLE_SHIFT = 0.5


def local(h_panel, s_panel, col_index, pattern, dinv, ainv_cc):
    panel_cols = h_panel - POLE_SHIFT * s_panel
    super_width = dinv.shape[0]
    received = lax.all_to_all(
        panel_cols, ("wide", "narrow"), split_axis=1, concat_axis=0, tiled=True
    )
    dinv_rows = jnp.take(dinv, col_index, axis=0)
    factor_panel = lax.dot_general(
        received,
        dinv_rows,
        (((0,), (0,)), ((), ())),
        precision=lax.Precision.HIGHEST,
        preferred_element_type=jnp.float32,
    )
    live_rows = (pattern > 0).astype(jnp.float32)
    factor_panel = (
        factor_panel.reshape(live_rows.shape[0], -1, super_width) * live_rows[:, None, None]
    ).reshape(factor_panel.shape)
    rows_here = ainv_cc.shape[0]
    inverse_flat = ainv_cc.reshape(rows_here, -1)
    partial_value = jnp.dot(
        inverse_flat,
        lax.all_gather(factor_panel, "wide", axis=0, tiled=True),
        precision=lax.Precision.HIGHEST,
        preferred_element_type=jnp.float32,
    )
    ainv_ck = -lax.psum_scatter(partial_value, "narrow", scatter_dimension=1, tiled=True)
    paired = lax.all_gather(factor_panel, "narrow", axis=0, tiled=True)
    corner_term = lax.dot_general(
        paired,
        ainv_ck,
        (((0,), (0,)), ((), ())),
        precision=lax.Precision.HIGHEST,
        preferred_element_type=jnp.float32,
    )
    summed = lax.psum_scatter(corner_term, "wide", scatter_dimension=0, tiled=True)
    half_width = ainv_ck.shape[1]
    rows_corner = summed.shape[0]
    corner = lax.dynamic_slice(
        dinv,
        (lax.axis_index("wide") * rows_corner, lax.axis_index("narrow") * half_width),
        (rows_corner, half_width),
    )
    return (ainv_ck, corner - summed)


def solution(mesh):
    placed = (
        P(("pole", "wide", "narrow"), None),
        P(("pole", "wide", "narrow"), None),
        P("pole"),
        P(("pole", "wide", "narrow")),
        P("pole", None),
        P(("pole", "wide"), None, "narrow", None),
    )
    return jax.shard_map(
        local,
        mesh=mesh,
        in_specs=placed,
        out_specs=(P(("pole", "wide"), "narrow"), P(("pole", "wide"), "narrow")),
        check_vma=False,
    )
```

profile of v0, /device:TPU:0, one launch (start us, length us, event | category | flops | bytes accessed | tf_op | source)
XLA Modules:
  0.0 148.3 jit_solution(7724145951328195672)
XLA Ops:
  7.2 0.0 copy-start
  7.2 1.7 %copy_bitcast_fusion = f32[16,16,128]{2,0,1:T(8,128)} fusion(f32[16,2048]{1,0:T(8,128)} %param.6, f32[16,2048]{1,0:T(8,128)} %param.7), kind=kLoop, calls=%fused_computation.7 | loop fusion | flops 65536 | bytes 393216 | tf_op jit(solution)/shard_map/all_to_all | solution.py:12
  8.9 0.0 copy-start.4
  8.9 7.5 %all-to-all-start = ((f32[16,16,128]{2,0,1:T(8,128)}), f32[16,16,128]{2,0,1:T(8,128)S(1)}, u32[]{:S(2)}, u32[]{:S(2)}) async-start(f32[16,16,128]{2,0,1:T(8,128)} %copy_bitcast_fusion), calls=%async_computation | async-start | bytes 262144 | tf_op jit(solution)/shard_map/all_to_all | solution.py:12
  16.4 0.0 copy-start.5
  16.4 0.0 all-gather.2.cloned.1.call-start
  16.5 0.0 copy-done.4
  16.5 0.6 copy-done.5
  17.1 0.0 copy-done
  17.1 0.0 copy-start.2
  17.1 1.0 gather_fusion
  18.1 6.2 %all-to-all-done = f32[16,16,128]{2,0,1:T(8,128)S(1)} async-done(((f32[16,16,128]{2,0,1:T(8,128)}), f32[16,16,128]{2,0,1:T(8,128)S(1)}, u32[]{:S(2)}, u32[]{:S(2)}) %all-to-all-start) | async-done | bytes 131104 | tf_op jit(solution)/shard_map/all_to_all | solution.py:12
  24.3 0.1 copy.16
  24.4 1.0 convolution_multiply_fusion
  25.4 0.0 all-gather.2.cloned.1.call-update
  25.5 0.0 reduce-scatter.3.cloned.1.call-start
  25.5 38.2 %all-gather.2.cloned.1.call-done = f32[1024,256]{1,0:T(8,128)} async-done(((f32[128,256]{1,0:T(8,128)}), f32[1024,256]{1,0:T(8,128)}) %all-gather.2.cloned.1.call-update) | async-done | bytes 1048592 | tf_op jit(solution)/shard_map/all_gather | solution.py:31
  63.7 0.0 copy-done.2
  63.7 3.8 %convolution_bitcast_fusion = f32[256,256]{0,1:T(8,128)} fusion(f32[1024,256]{1,0:T(8,128)} %all-gather.2.cloned.1.call-done, f32[32,8,8,128]{3,2,1,0:T(8,128)S(1)} %bitcast.28), kind=kOutput, calls=%fused_computation.1 | convolution fusion | flops 805306368 | bytes 2359296 | tf_op jit(solution)/shard_map/dot_general | solution.py:29
  67.5 0.0 copy-start.1
  67.5 0.0 reduce-scatter.3.cloned.1.call-update
  67.5 0.0 reduce-scatter.5.cloned.1.call-start
  67.5 0.8 copy-done.1
  68.4 2.0 %all_gather.7 = f32[256,256]{1,0:T(8,128)S(1)} all-gather(f32[128,256]{1,0:T(8,128)S(1)} %bitcast.27), channel_id=1, replica_groups=mesh['pole'=2,'wide'=8,'narrow'=2] {'narrow'}, dimensions={0}, use_global_device_ids=true | all-gather | bytes 393216 | tf_op jit(solution)/shard_map/all_gather | solution.py:36
  70.4 3.7 %reduce-scatter.3.cloned.1.call-done = f32[256,128]{0,1:T(8,128)} async-done(((f32[256,256]{0,1:T(8,128)}), f32[256,128]{0,1:T(8,128)}) %reduce-scatter.3.cloned.1.call-update) | async-done | bytes 131088 | tf_op jit(solution)/shard_map/reduce_scatter | solution.py:35
  74.1 2.2 %fusion.7 = f32[256,128]{1,0:T(8,128)} fusion(f32[256,256]{1,0:T(8,128)S(1)} %all_gather.7, f32[256,128]{0,1:T(8,128)} %reduce-scatter.3.cloned.1.call-done), kind=kOutput, calls=%fused_computation.17 | convolution fusion | flops 100696064 | bytes 524288 | tf_op jit(solution)/shard_map/dot_general | solution.py:37
  76.3 0.0 copy-start.3
  76.3 0.0 reduce-scatter.5.cloned.1.call-update
  76.3 0.9 copy-done.3
  77.2 0.8 copy.17
  77.9 62.5 %reduce-scatter.5.cloned.1.call-done = f32[32,128]{1,0:T(8,128)} async-done(((f32[256,128]{1,0:T(8,128)}), f32[32,128]{1,0:T(8,128)}) %reduce-scatter.5.cloned.1.call-update) | async-done | bytes 16400 | tf_op jit(solution)/shard_map/reduce_scatter | solution.py:44
  140.4 1.3 dynamic-slice_subtract_fusion
  (5 shorter events, 0.0 us)
Async XLA Ops:
  7.2 9.9 %copy-start = (f32[256,256]{1,0:T(8,128)S(1)}, f32[256,256]{1,0:T(8,128)}, u32[]{:S(2)}) copy-start(f32[256,256]{1,0:T(8,128)} %param.10) | copy-start | bytes 786436
  8.9 7.6 %copy-start.4 = (s32[256]{0:T(256)S(1)}, s32[256]{0:T(256)}, u32[]{:S(2)}) copy-start(s32[256]{0:T(256)} %param.8) | copy-start | bytes 3076
  8.9 15.5 %all-to-all-start = ((f32[16,16,128]{2,0,1:T(8,128)}), f32[16,16,128]{2,0,1:T(8,128)S(1)}, u32[]{:S(2)}, u32[]{:S(2)}) async-start(f32[16,16,128]{2,0,1:T(8,128)} %copy_bitcast_fusion), calls=%async_computation | async-start | bytes 262144 | tf_op jit(solution)/shard_map/all_to_all | solution.py:12
  16.4 0.7 copy-start.5
  16.4 47.2 %all-gather.2.cloned.1.call-start = ((), (), s32[]{:S(2)}) async-start(), calls=%async_computation.3 | async-start | bytes 1179648 | tf_op jit(solution)/shard_map/all_gather | solution.py:31
  17.1 46.6 %copy-start.2 = (f32[256,8,1,128]{3,2,1,0:T(1,128)S(1)}, f32[256,8,1,128]{3,2,1,0:T(1,128)}, u32[]{:S(2)}) copy-start(f32[256,8,1,128]{3,2,1,0:T(1,128)} %param.11) | copy-start | bytes 3145732
  25.5 48.6 %reduce-scatter.3.cloned.1.call-start = ((), (), s32[]{:S(2)}) async-start(), calls=%async_computation.4 | async-start | bytes 393216 | tf_op jit(solution)/shard_map/reduce_scatter | solution.py:35
  67.5 0.9 copy-start.1
  67.5 72.9 %reduce-scatter.5.cloned.1.call-start = ((), (), s32[]{:S(2)}) async-start(), calls=%async_computation.5 | async-start | bytes 147456 | tf_op jit(solution)/shard_map/reduce_scatter | solution.py:44
  76.3 0.9 copy-start.3
Sparse Core Ops, SparseCore 0:
  25.6 38.0 all-gather.1
  67.6 6.4 reduce-scatter.2
  77.4 62.9 reduce-scatter.4
where the time goes:
time: 149 us; the launch traced here: 148 us
  waiting for transfers between devices  111 us (74%)
  between operations  13.8 us (9%)
  starting transfers between devices  7.67 us (5%)
  matrix products  6.98 us (5%)
  local copies, waits for them, and re-layouts  4.11 us (3%)
  other arithmetic  3.04 us (2%)
  blocking collectives  1.98 us (1%)
    reduce_scatter x1, waiting for transfers between devices, local(): lax.psum_scatter(corner_term, 'wide', scatter_dimension=0, tiled=True)  62.5 us
    all_gather x1, waiting for transfers between devices, local(): lax.all_gather(factor_panel, 'wide', axis=0, tiled=True)  38.2 us
    all_to_all x1, starting transfers between devices, local(): lax.all_to_all(panel_cols, ('wide', 'narrow'), split_axis=1, concat_axis=...  7.55 us
    all_to_all x1, waiting for transfers between devices, local(): lax.all_to_all(panel_cols, ('wide', 'narrow'), split_axis=1, concat_axis=...  6.22 us
    dot_general x1, matrix products, local(): jnp.dot(inverse_flat, lax.all_gather(factor_panel, 'wide', axis=0, tiled=...  3.8 us
    reduce_scatter x1, waiting for transfers between devices, local(): lax.psum_scatter(partial_value, 'narrow', scatter_dimension=1, tiled=True)  3.75 us
    unnamed x13, local copies, waits for them, and re-layouts  3.05 us
  transfers between devices with their start and end apart: 4, of which 4 were waited for; matrix products, arithmetic and copies ran while one was open for 1% of the time, Pallas kernels for 0%

commit v1 on v0

--- a/solution.py
+++ b/solution.py
@@ -2,6 +2,7 @@
 import jax.numpy as jnp
 from jax import lax
 from jax.sharding import PartitionSpec as P
+from jax.lax import all_to_all, axis_size
 
 POLE_SHIFT = 0.5
 
@@ -9,8 +10,14 @@
 def local(h_panel, s_panel, col_index, pattern, dinv, ainv_cc):
     panel_cols = h_panel - POLE_SHIFT * s_panel
     super_width = dinv.shape[0]
-    received = lax.all_to_all(
-        panel_cols, ("wide", "narrow"), split_axis=1, concat_axis=0, tiled=True
+    received = jnp.concatenate(
+        all_to_all(
+            jnp.stack(jnp.split(panel_cols, axis_size(("wide", "narrow")), axis=1)),
+            axis_name=("wide", "narrow"),
+            concat_axis=0,
+            split_axis=0,
+        ),
+        0,
     )
     dinv_rows = jnp.take(dinv, col_index, axis=0)
     factor_panel = lax.dot_general(

time: 149 us -> 158 us (1.060)
  local copies, waits for them, and re-layouts: 4.11 us -> 13.7 us
    unnamed x13 -> x28, local copies, waits for them, and re-layouts: 3.05 us -> 12 us
    all_to_all x1 -> x0, other arithmetic: 1.68 us -> none  [local(): lax.all_to_all(panel_cols, ('wide', 'narrow'), split_axis=1, concat_axis=...]
where the time goes in v1:
time: 158 us; the launch traced here: 157 us
  waiting for transfers between devices  111 us (70%)
  between operations  13.8 us (9%)
  local copies, waits for them, and re-layouts  13.7 us (9%)
  starting transfers between devices  7.67 us (5%)
  matrix products  6.98 us (4%)
  other arithmetic  2.34 us (1%)
  blocking collectives  1.98 us (1%)
    reduce_scatter x1, waiting for transfers between devices, local(): lax.psum_scatter(corner_term, 'wide', scatter_dimension=0, tiled=True)  62.5 us
    all_gather x1, waiting for transfers between devices, local(): lax.all_gather(factor_panel, 'wide', axis=0, tiled=True)  38.2 us
    unnamed x28, local copies, waits for them, and re-layouts  12 us
    all_to_all x1, starting transfers between devices, local(): all_to_all(jnp.stack(jnp.split(panel_cols, axis_size(('wide', 'narrow')),...  7.55 us
    all_to_all x1, waiting for transfers between devices, local(): all_to_all(jnp.stack(jnp.split(panel_cols, axis_size(('wide', 'narrow')),...  6.22 us
    dot_general x1, matrix products, local(): jnp.dot(inverse_flat, lax.all_gather(factor_panel, 'wide', axis=0, tiled=...  3.8 us
    reduce_scatter x1, waiting for transfers between devices, local(): lax.psum_scatter(partial_value, 'narrow', scatter_dimension=1, tiled=True)  3.75 us
  transfers between devices with their start and end apart: 4, of which 4 were waited for; matrix products, arithmetic and copies ran while one was open for 1% of the time, Pallas kernels for 0%

profile of v1, /device:TPU:0, one launch (start us, length us, event | category | flops | bytes accessed | tf_op | source)
XLA Modules:
  0.0 157.2 jit_solution(12368213506509311730)
XLA Ops:
  7.2 1.0 multiply_subtract_fusion
  8.2 0.6 constant_dynamic-update-slice_fusion.15
  8.8 0.6 constant_dynamic-update-slice_fusion.14
  9.4 0.6 constant_dynamic-update-slice_fusion.13
  10.0 0.6 constant_dynamic-update-slice_fusion.12
  10.6 0.6 constant_dynamic-update-slice_fusion.11
  11.2 0.6 constant_dynamic-update-slice_fusion.10
  11.8 0.6 constant_dynamic-update-slice_fusion.9
  12.4 0.6 constant_dynamic-update-slice_fusion.8
  13.0 0.6 constant_dynamic-update-slice_fusion.7
  13.6 0.6 constant_dynamic-update-slice_fusion.6
  14.2 0.6 constant_dynamic-update-slice_fusion.5
  14.8 0.6 constant_dynamic-update-slice_fusion.4
  15.4 0.6 constant_dynamic-update-slice_fusion.3
  16.0 0.6 constant_dynamic-update-slice_fusion.2
  16.6 0.6 constant_dynamic-update-slice_fusion.1
  17.2 0.6 constant_dynamic-update-slice_fusion
  17.8 7.5 %all-to-all-start = ((f32[16,16,128]{2,1,0:T(8,128)}), f32[16,16,128]{2,1,0:T(8,128)S(1)}, u32[]{:S(2)}, u32[]{:S(2)}) async-start(f32[16,16,128]{2,1,0:T(8,128)} %constant_dynamic-update-slice_fusion), calls=%async_computation | async-start | bytes 262144 | tf_op jit(solution)/shard_map/all_to_all | solution.py:14
  25.4 0.6 copy-done.5
  26.0 1.0 gather_fusion
  27.0 6.2 %all-to-all-done = f32[16,16,128]{2,1,0:T(8,128)S(1)} async-done(((f32[16,16,128]{2,1,0:T(8,128)}), f32[16,16,128]{2,1,0:T(8,128)S(1)}, u32[]{:S(2)}, u32[]{:S(2)}) %all-to-all-start) | async-done | bytes 131104 | tf_op jit(solution)/shard_map/all_to_all | solution.py:14
  33.3 1.0 convolution_multiply_fusion
  34.4 38.2 %all-gather.2.cloned.1.call-done = f32[1024,256]{1,0:T(8,128)} async-done(((f32[128,256]{1,0:T(8,128)}), f32[1024,256]{1,0:T(8,128)}) %all-gather.2.cloned.1.call-update) | async-done | bytes 1048592 | tf_op jit(solution)/shard_map/all_gather | solution.py:38
  72.6 3.8 %convolution_bitcast_fusion = f32[256,256]{0,1:T(8,128)} fusion(f32[1024,256]{1,0:T(8,128)} %all-gather.2.cloned.1.call-done, f32[32,8,8,128]{3,2,1,0:T(8,128)S(1)} %bitcast.85), kind=kOutput, calls=%fused_computation.1 | convolution fusion | flops 805306368 | bytes 2359296 | tf_op jit(solution)/shard_map/dot_general | solution.py:36
  76.4 0.8 copy-done.1
  77.3 2.0 %all_gather.7 = f32[256,256]{1,0:T(8,128)S(1)} all-gather(f32[128,256]{1,0:T(8,128)S(1)} %bitcast.84), channel_id=1, replica_groups=mesh['pole'=2,'wide'=8,'narrow'=2] {'narrow'}, dimensions={0}, use_global_device_ids=true | all-gather | bytes 393216 | tf_op jit(solution)/shard_map/all_gather | solution.py:43
  79.3 3.7 %reduce-scatter.3.cloned.1.call-done = f32[256,128]{0,1:T(8,128)} async-done(((f32[256,256]{0,1:T(8,128)}), f32[256,128]{0,1:T(8,128)}) %reduce-scatter.3.cloned.1.call-update) | async-done | bytes 131088 | tf_op jit(solution)/shard_map/reduce_scatter | solution.py:42
  83.0 2.2 %fusion.7 = f32[256,128]{1,0:T(8,128)} fusion(f32[256,256]{1,0:T(8,128)S(1)} %all_gather.7, f32[256,128]{0,1:T(8,128)} %reduce-scatter.3.cloned.1.call-done), kind=kOutput, calls=%fused_computation.48 | convolution fusion | flops 100696064 | bytes 524288 | tf_op jit(solution)/shard_map/dot_general | solution.py:44
  85.2 0.9 copy-done.3
  86.1 0.8 copy.9
  86.8 62.5 %reduce-scatter.5.cloned.1.call-done = f32[32,128]{1,0:T(8,128)} async-done(((f32[256,128]{1,0:T(8,128)}), f32[32,128]{1,0:T(8,128)}) %reduce-scatter.5.cloned.1.call-update) | async-done | bytes 16400 | tf_op jit(solution)/shard_map/reduce_scatter | solution.py:51
  149.4 1.3 dynamic-slice_subtract_fusion
  (21 shorter events, 0.3 us)
Async XLA Ops:
  8.8 17.2 %copy-start = (f32[256,256]{1,0:T(8,128)S(1)}, f32[256,256]{1,0:T(8,128)}, u32[]{:S(2)}) copy-start(f32[256,256]{1,0:T(8,128)} %param.10) | copy-start | bytes 786436
  17.8 7.6 %copy-start.4 = (s32[256]{0:T(256)S(1)}, s32[256]{0:T(256)}, u32[]{:S(2)}) copy-start(s32[256]{0:T(256)} %param.8) | copy-start | bytes 3076
  17.8 15.5 %all-to-all-start = ((f32[16,16,128]{2,1,0:T(8,128)}), f32[16,16,128]{2,1,0:T(8,128)S(1)}, u32[]{:S(2)}, u32[]{:S(2)}) async-start(f32[16,16,128]{2,1,0:T(8,128)} %constant_dynamic-update-slice_fusion), calls=%async_computation | async-start | bytes 262144 | tf_op jit(solution)/shard_map/all_to_all | solution.py:14
  25.3 0.7 copy-start.5
  25.3 47.2 %all-gather.2.cloned.1.call-start = ((), (), s32[]{:S(2)}) async-start(), calls=%async_computation.3 | async-start | bytes 1179648 | tf_op jit(solution)/shard_map/all_gather | solution.py:38
  26.0 46.6 %copy-start.2 = (f32[256,8,1,128]{3,2,1,0:T(1,128)S(1)}, f32[256,8,1,128]{3,2,1,0:T(1,128)}, u32[]{:S(2)}) copy-start(f32[256,8,1,128]{3,2,1,0:T(1,128)} %param.11) | copy-start | bytes 3145732
  34.4 48.6 %reduce-scatter.3.cloned.1.call-start = ((), (), s32[]{:S(2)}) async-start(), calls=%async_computation.4 | async-start | bytes 393216 | tf_op jit(solution)/shard_map/reduce_scatter | solution.py:42
  76.4 0.9 copy-start.1
  76.4 73.0 %reduce-scatter.5.cloned.1.call-start = ((), (), s32[]{:S(2)}) async-start(), calls=%async_computation.5 | async-start | bytes 147456 | tf_op jit(solution)/shard_map/reduce_scatter | solution.py:51
  85.2 0.9 copy-start.3
Sparse Core Ops, SparseCore 0:
  34.5 38.0 all-gather.1
  76.5 6.4 reduce-scatter.2
  86.3 62.9 reduce-scatter.4

commit v2 on v0

--- a/solution.py
+++ b/solution.py
@@ -26,9 +26,18 @@
     ).reshape(factor_panel.shape)
     rows_here = ainv_cc.shape[0]
     inverse_flat = ainv_cc.reshape(rows_here, -1)
+
+    def switch_cycles(packet):
+        return jnp.concatenate(
+            lax.all_to_all(
+                jnp.stack(tuple((packet for _ in range(lax.axis_size("wide"))))), "wide", 0, 0
+            ),
+            axis=0,
+        )
+
     partial_value = jnp.dot(
         inverse_flat,
-        lax.all_gather(factor_panel, "wide", axis=0, tiled=True),
+        switch_cycles(factor_panel),
         precision=lax.Precision.HIGHEST,
         preferred_element_type=jnp.float32,
     )

time: 149 us -> 138 us (0.926)
  waiting for transfers between devices: 111 us -> 73.6 us
  blocking collectives: 1.98 us -> 30.3 us
  matrix products: 6.98 us -> 5.09 us
    all_gather x1 -> x0, waiting for transfers between devices: 38.2 us -> none  [local(): lax.all_gather(factor_panel, 'wide', axis=0, tiled=True)]
    all_to_all x0 -> x1, blocking collectives: none -> 28.3 us  [switch_cycles(): lax.all_to_all(jnp.stack(tuple((packet for _ in range(lax.axis_size('wide...]
    unnamed x13 -> x11, local copies, waits for them, and re-layouts: 3.05 us -> 2.22 us
  transfers between devices with their start and end apart: 4 -> 3, of which waited for: 4 -> 3; matrix products, arithmetic and copies ran while one was open for 1% -> 1% of each run, Pallas kernels for 0% -> 0%
where the time goes in v2:
time: 138 us; the launch traced here: 137 us
  waiting for transfers between devices  73.6 us (53%)
  blocking collectives  30.3 us (22%)
  between operations  14.1 us (10%)
  starting transfers between devices  7.63 us (6%)
  matrix products  5.09 us (4%)
  local copies, waits for them, and re-layouts  3.37 us (2%)
  other arithmetic  3.04 us (2%)
    reduce_scatter x1, waiting for transfers between devices, local(): lax.psum_scatter(corner_term, 'wide', scatter_dimension=0, tiled=True)  62.5 us
    all_to_all x1, blocking collectives, switch_cycles(): lax.all_to_all(jnp.stack(tuple((packet for _ in range(lax.axis_size('wide...  28.3 us
    all_to_all x1, starting transfers between devices, local(): lax.all_to_all(panel_cols, ('wide', 'narrow'), split_axis=1, concat_axis=...  7.55 us
    all_to_all x1, waiting for transfers between devices, local(): lax.all_to_all(panel_cols, ('wide', 'narrow'), split_axis=1, concat_axis=...  6.24 us
    reduce_scatter x1, waiting for transfers between devices, local(): lax.psum_scatter(partial_value, 'narrow', scatter_dimension=1, tiled=True)  4.84 us
  transfers between devices with their start and end apart: 3, of which 3 were waited for; matrix products, arithmetic and copies ran while one was open for 1% of the time, Pallas kernels for 0%

profile of v2, /device:TPU:0, one launch (start us, length us, event | category | flops | bytes accessed | tf_op | source)
XLA Modules:
  0.0 137.2 jit_solution(650887902012885658)
XLA Ops:
  7.2 0.0 copy-start
  7.2 1.7 %copy_bitcast_fusion = f32[16,16,128]{2,0,1:T(8,128)} fusion(f32[16,2048]{1,0:T(8,128)} %param.6, f32[16,2048]{1,0:T(8,128)} %param.7), kind=kLoop, calls=%fused_computation.7 | loop fusion | flops 65536 | bytes 393216 | tf_op jit(solution)/shard_map/all_to_all | solution.py:12
  8.9 0.0 copy-start.3
  8.9 7.5 %all-to-all-start = ((f32[16,16,128]{2,0,1:T(8,128)}), f32[16,16,128]{2,0,1:T(8,128)S(1)}, u32[]{:S(2)}, u32[]{:S(2)}) async-start(f32[16,16,128]{2,0,1:T(8,128)} %copy_bitcast_fusion), calls=%async_computation | async-start | bytes 262144 | tf_op jit(solution)/shard_map/all_to_all | solution.py:12
  16.4 0.0 copy-start.4
  16.4 0.0 reduce-scatter.3.cloned.1.call-start
  16.5 0.0 copy-done.3
  16.5 0.6 copy-done.4
  17.1 0.0 copy-done
  17.1 1.0 gather_fusion
  18.1 6.2 %all-to-all-done = f32[16,16,128]{2,0,1:T(8,128)S(1)} async-done(((f32[16,16,128]{2,0,1:T(8,128)}), f32[16,16,128]{2,0,1:T(8,128)S(1)}, u32[]{:S(2)}, u32[]{:S(2)}) %all-to-all-start) | async-done | bytes 131104 | tf_op jit(solution)/shard_map/all_to_all | solution.py:12
  24.3 0.1 copy.16
  24.4 0.4 convolution_multiply_fusion
  24.8 0.1 stack.3
  24.9 0.0 copy-start.1
  24.9 28.3 %all_to_all.24 = f32[8,128,256]{2,1,0:T(8,128)S(1)} all-to-all(f32[8,128,256]{2,1,0:T(8,128)S(1)} %stack.3), channel_id=1, replica_groups=mesh['pole'=2,'wide'=8,'narrow'=2] {'wide'}, dimensions={0} | all-to-all | bytes 2097152 | tf_op jit(solution)/shard_map/all_to_all | solution.py:32
  53.2 0.0 copy-done.1
  53.2 2.6 %convolution_bitcast_fusion = f32[256,256]{0,1:T(8,128)} fusion(f32[1024,256]{1,0:T(8,128)S(1)} %bitcast.27, f32[32,8,8,128]{3,2,1,0:T(8,128)S(1)} %bitcast.30), kind=kOutput, calls=%fused_computation.1 | convolution fusion | flops 805306368 | bytes 2359296 | tf_op jit(solution)/shard_map/dot_general | solution.py:38
  55.8 0.0 reduce-scatter.3.cloned.1.call-update
  55.8 0.0 reduce-scatter.5.cloned.1.call-start
  55.9 2.0 %all_gather.3 = f32[256,256]{1,0:T(8,128)S(1)} all-gather(f32[128,256]{1,0:T(8,128)S(1)} %bitcast.29), channel_id=1, replica_groups=mesh['pole'=2,'wide'=8,'narrow'=2] {'narrow'}, dimensions={0}, use_global_device_ids=true | all-gather | bytes 393216 | tf_op jit(solution)/shard_map/all_gather | solution.py:45
  57.9 4.8 %reduce-scatter.3.cloned.1.call-done = f32[256,128]{0,1:T(8,128)} async-done(((f32[256,256]{0,1:T(8,128)}), f32[256,128]{0,1:T(8,128)}) %reduce-scatter.3.cloned.1.call-update) | async-done | bytes 131088 | tf_op jit(solution)/shard_map/reduce_scatter | solution.py:44
  62.7 2.1 %fusion.7 = f32[256,128]{1,0:T(8,128)} fusion(f32[256,256]{1,0:T(8,128)S(1)} %all_gather.3, f32[256,128]{0,1:T(8,128)} %reduce-scatter.3.cloned.1.call-done), kind=kOutput, calls=%fused_computation.17 | convolution fusion | flops 100696064 | bytes 524288 | tf_op jit(solution)/shard_map/dot_general | solution.py:46
  64.9 0.0 copy-start.2
  64.9 0.0 reduce-scatter.5.cloned.1.call-update
  64.9 0.9 copy-done.2
  65.8 0.8 copy.17
  66.5 62.5 %reduce-scatter.5.cloned.1.call-done = f32[32,128]{1,0:T(8,128)} async-done(((f32[256,128]{1,0:T(8,128)}), f32[32,128]{1,0:T(8,128)}) %reduce-scatter.5.cloned.1.call-update) | async-done | bytes 16400 | tf_op jit(solution)/shard_map/reduce_scatter | solution.py:53
  129.0 1.3 dynamic-slice_subtract_fusion
  (5 shorter events, 0.0 us)
Async XLA Ops:
  7.2 9.9 %copy-start = (f32[256,256]{1,0:T(8,128)S(1)}, f32[256,256]{1,0:T(8,128)}, u32[]{:S(2)}) copy-start(f32[256,256]{1,0:T(8,128)} %param.10) | copy-start | bytes 786436
  8.9 7.6 %copy-start.3 = (s32[256]{0:T(256)S(1)}, s32[256]{0:T(256)}, u32[]{:S(2)}) copy-start(s32[256]{0:T(256)} %param.8) | copy-start | bytes 3076
  8.9 15.5 %all-to-all-start = ((f32[16,16,128]{2,0,1:T(8,128)}), f32[16,16,128]{2,0,1:T(8,128)S(1)}, u32[]{:S(2)}, u32[]{:S(2)}) async-start(f32[16,16,128]{2,0,1:T(8,128)} %copy_bitcast_fusion), calls=%async_computation | async-start | bytes 262144 | tf_op jit(solution)/shard_map/all_to_all | solution.py:12
  16.4 0.7 copy-start.4
  16.4 46.3 %reduce-scatter.3.cloned.1.call-start = ((), (), s32[]{:S(2)}) async-start(), calls=%async_computation.4 | async-start | bytes 393216 | tf_op jit(solution)/shard_map/reduce_scatter | solution.py:44
  24.9 28.3 %copy-start.1 = (f32[256,8,1,128]{3,2,1,0:T(1,128)S(1)}, f32[256,8,1,128]{3,2,1,0:T(1,128)}, u32[]{:S(2)}) copy-start(f32[256,8,1,128]{3,2,1,0:T(1,128)} %param.11) | copy-start | bytes 3145732
  55.8 73.2 %reduce-scatter.5.cloned.1.call-start = ((), (), s32[]{:S(2)}) async-start(), calls=%async_computation.5 | async-start | bytes 147456 | tf_op jit(solution)/shard_map/reduce_scatter | solution.py:53
  64.9 0.9 copy-start.2
Sparse Core Ops, SparseCore 0:
  55.9 6.7 reduce-scatter.2
  66.0 62.9 reduce-scatter.4
